TPU v7x, 32 devices: a whole 2x2x4 slice. The times are simulated.
32 devices in a mesh: row: 2 (over x), col: 4 (over y, core), rhs: 4 (over z).
Axes of the slice: x: 2, y: 2, z: 4, core: 2. Of those that a mesh axis runs over, the one named last changes fastest.
Arguments:
- right_side: float32 [2, 64, 8192], P('row', 'rhs', 'col'), may hold values from -6 to 6
- guess: float32 [2, 64, 8192], P('row', 'rhs', 'col'), may hold values from -6 to 6
- inverse: bfloat16 [2, 8192, 8192], P('row', 'rhs', 'col'), may hold values from -0.0625 to 0.0625
- left_factor: bfloat16 [2, 2, 64, 8192], P('row', None, None, 'col'), may hold values from -0.5 to 0.5
- right_factor: bfloat16 [2, 2, 64, 8192], P('row', None, None, 'col'), may hold values from -0.0625 to 0.0625
- ranks: int32 [2, 2], replicated, may hold values from 16 to 64
Outputs:
- solution: float32 [2, 64, 8192], P('row', 'rhs', 'col')
Inputs may be any that keep to these rules, and one draw needn't show every extreme that they name: ranks[i, j] is the rank of the block in block row i and block column j; diagonal entries are not read.
All inputs are finite; a program needn't handle non-finite values.
Results may differ from a plain program's by a relative error of at most 0.008.
Values may be sent and summed in bfloat16 or wider, within the bound.
A program may use at most 128 MiB of HBM per device.

v0:
```python
import jax
import jax.numpy as jnp
from jax import lax
from jax.sharding import PartitionSpec as P


def body(right_side, guess, inverse, left_factor, right_factor, ranks):
    blocks = lax.axis_size("row")
    mine = lax.axis_index("row")
    left = left_factor[0]
    right = right_factor[0]
    width = left.shape[1]
    keep = (lax.broadcasted_iota(jnp.int32, (blocks, blocks, width), 2) < ranks[:, :, None]).astype(
        jnp.float32
    )
    keep_mine = lax.dynamic_index_in_dim(keep, mine, 1, keepdims=False)
    partial_value = jnp.einsum(
        "rm,ikm->irk", guess[0].astype(jnp.bfloat16), right, preferred_element_type=jnp.float32
    )
    partial_value = partial_value * keep_mine[:, None, :]
    old_sum = lax.psum(partial_value, "col").astype(jnp.bfloat16)
    old_mine = lax.all_to_all(old_sum, "row", split_axis=0, concat_axis=0, tiled=True)
    later = lax.broadcasted_iota(jnp.int32, (blocks, 1, 1), 0) > mine
    old_kept = jnp.where(later, old_mine, jnp.zeros_like(old_mine))
    upper = jnp.einsum("jrk,jkm->rm", old_kept, left, preferred_element_type=jnp.float32)
    base = right_side[0] - upper
    lower = jnp.zeros_like(base)
    solution = jnp.zeros_like(base)
    for step in range(blocks):
        residue = (base - lower).astype(jnp.bfloat16)
        residue_full = lax.all_gather(residue, "col", axis=1, tiled=True)
        pieces = lax.all_to_all(residue_full, "rhs", split_axis=1, concat_axis=0, tiled=True)
        product = jnp.dot(pieces, inverse[0], preferred_element_type=jnp.float32)
        current = lax.psum_scatter(product, "rhs", scatter_dimension=0, tiled=True)
        solution = jnp.where(mine == step, current, solution)
        if step + 1 < blocks:
            coef = jnp.einsum(
                "rm,ikm->irk",
                current.astype(jnp.bfloat16),
                right,
                preferred_element_type=jnp.float32,
            )
            coef = coef * keep[:, step][:, None, :]
            coef = jnp.where(mine == step, coef, jnp.zeros_like(coef))
            shared = lax.psum(coef, ("row", "col")).astype(jnp.bfloat16)
            own_coef = lax.dynamic_index_in_dim(shared, mine, 0, keepdims=False)
            term = jnp.dot(own_coef, left[step], preferred_element_type=jnp.float32)
            lower = lower + jnp.where(mine > step, term, jnp.zeros_like(term))
    return solution[None]


def solution(mesh):
    in_specs = (
        P("row", "rhs", "col"),
        P("row", "rhs", "col"),
        P("row", "rhs", "col"),
        P("row", None, None, "col"),
        P("row", None, None, "col"),
        P(),
    )
    out_specs = P("row", "rhs", "col")
    return jax.shard_map(body, mesh=mesh, in_specs=in_specs, out_specs=out_specs, check_vma=False)
```

profile of v0, /device:TPU:0, one launch (start us, length us, event | category | flops | bytes accessed | tf_op | source)
XLA Modules:
  0.0 150.5 jit_solution(729392228866643291)
XLA Ops:
  6.5 0.0 copy-start
  6.5 0.8 copy.8
  7.4 0.1 compare_convert_fusion
  7.4 0.2 copy-done
  7.6 1.2 fusion.9
  8.8 12.7 %psum.14 = bf16[2,16,64]{2,1,0:T(8,128)(2,1)S(1)} all-reduce(f32[2,16,64]{2,1,0:T(8,128)S(1)} %fusion.9), channel_id=1, replica_groups=mesh['row'=2,'col'=4,'rhs'=4] {'col'}, use_global_device_ids=true, to_apply=%region_0.1 | all-reduce | flops 2048 | bytes 12288 | tf_op jit(solution)/shard_map/psum | solution.py:21
  21.5 0.7 reshape.18
  22.2 3.2 %all-to-all-start = ((bf16[2,2,512]{2,1,0:T(2,128)(2,1)}), bf16[2,2,512]{2,1,0:T(2,128)(2,1)S(1)}, u32[]{:S(2)}, u32[]{:S(2)}) async-start(bf16[2,2,512]{2,1,0:T(2,128)(2,1)} %reshape.18), calls=%async_computation | async-start | bytes 8192 | tf_op jit(solution)/shard_map/all_to_all | solution.py:22
  25.4 0.0 reduce-scatter.3.cloned.1.call-start
  25.5 3.7 %all-to-all-done = bf16[2,2,512]{2,1,0:T(2,128)(2,1)S(1)} async-done(((bf16[2,2,512]{2,1,0:T(2,128)(2,1)}), bf16[2,2,512]{2,1,0:T(2,128)(2,1)S(1)}, u32[]{:S(2)}, u32[]{:S(2)}) %all-to-all-start) | async-done | bytes 4128 | tf_op jit(solution)/shard_map/all_to_all | solution.py:22
  29.2 0.1 reshape.19
  29.3 1.4 fusion.26
  30.7 5.8 %all_gather.6 = bf16[16,8192]{1,0:T(8,128)(2,1)S(1)} all-gather(bf16[16,2048]{1,0:T(8,128)(2,1)S(1)} %get-tuple-element.7), channel_id=1, replica_groups=mesh['row'=2,'col'=4,'rhs'=4] {'col'}, dimensions={1}, use_global_device_ids=true | all-gather | bytes 327680 | tf_op jit(solution)/shard_map/all_gather | solution.py:31
  36.5 14.1 %all_to_all.43 = bf16[16,4,2048]{2,0,1:T(8,128)(2,1)S(1)} all-to-all(bf16[16,4,2048]{2,0,1:T(8,128)(2,1)S(1)} %bitcast.64), channel_id=1, replica_groups=mesh['row'=2,'col'=4,'rhs'=4] {'rhs'}, dimensions={1} | all-to-all | bytes 524288 | tf_op jit(solution)/shard_map/all_to_all | solution.py:32
  50.5 0.0 copy-start.1
  50.5 5.8 %fusion.2 = f32[64,2048]{1,0:T(8,128)} fusion(bf16[64,2048]{1,0:T(8,128)(2,1)S(1)} %bitcast.60, bf16[1,2048,2048]{2,1,0:T(8,128)(2,1)} %param.8), kind=kOutput, calls=%fused_computation.2 | convolution fusion | flops 536870912 | bytes 9175040 | tf_op jit(solution)/shard_map/dot_general | solution.py:33
  56.3 0.0 reduce-scatter.3.cloned.1.call-update
  56.4 0.0 reduce-scatter.5.cloned.1.call-start
  56.4 19.2 %reduce-scatter.3.cloned.1.call-done = f32[16,2048]{1,0:T(8,128)} async-done(((f32[64,2048]{1,0:T(8,128)}), f32[16,2048]{1,0:T(8,128)}) %reduce-scatter.3.cloned.1.call-update) | async-done | bytes 131088 | tf_op jit(solution)/shard_map/reduce_scatter | solution.py:34
  75.6 1.2 fusion.8
  76.8 22.3 %psum.15 = bf16[2,16,64]{2,1,0:T(8,128)(2,1)S(1)} all-reduce(f32[2,16,64]{2,1,0:T(8,128)S(1)} %fusion.8), channel_id=1, replica_groups=mesh['row'=2,'col'=4,'rhs'=4] {'row','col'}, use_global_device_ids=true, to_apply=%region_2.3 | all-reduce | flops 2048 | bytes 12288 | tf_op jit(solution)/shard_map/psum | solution.py:45
  99.2 0.0 copy-done.1
  99.2 0.2 fusion.6
  99.3 5.8 %all_gather.7 = bf16[16,8192]{1,0:T(8,128)(2,1)S(1)} all-gather(bf16[16,2048]{1,0:T(8,128)(2,1)S(1)} %fusion.6), channel_id=1, replica_groups=mesh['row'=2,'col'=4,'rhs'=4] {'col'}, dimensions={1}, use_global_device_ids=true | all-gather | bytes 327680 | tf_op jit(solution)/shard_map/all_gather | solution.py:31
  105.1 12.0 %all_to_all.44 = bf16[16,4,2048]{2,0,1:T(8,128)(2,1)S(1)} all-to-all(bf16[16,4,2048]{2,0,1:T(8,128)(2,1)S(1)} %bitcast.65), channel_id=1, replica_groups=mesh['row'=2,'col'=4,'rhs'=4] {'rhs'}, dimensions={1} | all-to-all | bytes 524288 | tf_op jit(solution)/shard_map/all_to_all | solution.py:32
  117.2 0.0 copy-start.2
  117.2 5.8 %fusion = f32[64,2048]{1,0:T(8,128)} fusion(bf16[64,2048]{1,0:T(8,128)(2,1)S(1)} %bitcast.61, bf16[1,2048,2048]{2,1,0:T(8,128)(2,1)} %param.8), kind=kOutput, calls=%fused_computation | convolution fusion | flops 536870912 | bytes 9175040 | tf_op jit(solution)/shard_map/dot_general | solution.py:33
  122.9 0.0 reduce-scatter.5.cloned.1.call-update
  123.0 20.0 %reduce-scatter.5.cloned.1.call-done = f32[16,2048]{1,0:T(8,128)} async-done(((f32[64,2048]{1,0:T(8,128)}), f32[16,2048]{1,0:T(8,128)}) %reduce-scatter.5.cloned.1.call-update) | async-done | bytes 131088 | tf_op jit(solution)/shard_map/reduce_scatter | solution.py:34
  143.0 0.0 copy-done.2
  143.0 0.7 select_bitcast_fusion
  (4 shorter events, 0.0 us)
Async XLA Ops:
  6.5 1.1 copy-start
  22.2 7.0 %all-to-all-start = ((bf16[2,2,512]{2,1,0:T(2,128)(2,1)}), bf16[2,2,512]{2,1,0:T(2,128)(2,1)S(1)}, u32[]{:S(2)}, u32[]{:S(2)}) async-start(bf16[2,2,512]{2,1,0:T(2,128)(2,1)} %reshape.18), calls=%async_computation | async-start | bytes 8192 | tf_op jit(solution)/shard_map/all_to_all | solution.py:22
  25.4 50.2 %reduce-scatter.3.cloned.1.call-start = ((), (), s32[]{:S(2)}) async-start(), calls=%async_computation.5 | async-start | bytes 655360 | tf_op jit(solution)/shard_map/reduce_scatter | solution.py:34
  50.5 48.6 %copy-start.1 = (bf16[1,2,64,2048]{3,2,1,0:T(8,128)(2,1)S(1)}, bf16[1,2,64,2048]{3,2,1,0:T(8,128)(2,1)}, u32[]{:S(2)}) copy-start(bf16[1,2,64,2048]{3,2,1,0:T(8,128)(2,1)} %param.9) | copy-start | bytes 1572868
  56.4 86.6 %reduce-scatter.5.cloned.1.call-start = ((), (), s32[]{:S(2)}) async-start(), calls=%async_computation.6 | async-start | bytes 655360 | tf_op jit(solution)/shard_map/reduce_scatter | solution.py:34
  117.2 25.8 %copy-start.2 = (f32[16,2048]{1,0:T(8,128)S(1)}, f32[16,2048]{1,0:T(8,128)}, u32[]{:S(2)}) copy-start(f32[16,2048]{1,0:T(8,128)} %reduce-scatter.3.cloned.1.call-done) | copy-start | bytes 393220
Sparse Core Ops, SparseCore 0:
  56.5 19.0 reduce-scatter.2
  123.1 19.8 reduce-scatter.4
where the time goes:
time: 151 us
  blocking collectives  72.7 us (48%)
  waiting for transfers between devices  43 us (28%)
  matrix products  15.5 us (10%)
  between operations  13.4 us (9%)
  starting transfers between devices  3.3 us (2%)
  local copies, waits for them, and re-layouts  1.79 us (1%)
    reduce_scatter x2, waiting for transfers between devices, body(): current = lax.psum_scatter(product, 'rhs', scatter_dimension=0, tiled=True)  39.2 us
    all_to_all x2, blocking collectives, body(): lax.all_to_all(residue_full, 'rhs', split_axis=1, concat_axis=0, tiled=True)  26.1 us
    psum x1, blocking collectives, body(): shared = lax.psum(coef, ('row', 'col')).astype(jnp.bfloat16)  22.3 us
    psum x1, blocking collectives, body(): old_sum = lax.psum(partial_value, 'col').astype(jnp.bfloat16)  12.7 us
    dot_general x2, matrix products, body(): product = jnp.dot(pieces, inverse[0], preferred_element_type=jnp.float32)  11.6 us
    all_gather x2, blocking collectives, body(): residue_full = lax.all_gather(residue, 'col', axis=1, tiled=True)  11.6 us
    all_to_all x1, waiting for transfers between devices, body(): lax.all_to_all(old_sum, 'row', split_axis=0, concat_axis=0, tiled=True)  3.71 us
    all_to_all x1, starting transfers between devices, body(): lax.all_to_all(old_sum, 'row', split_axis=0, concat_axis=0, tiled=True)  3.22 us
  transfers between devices with their start and end apart: 3, of which 3 were waited for; matrix products, arithmetic and copies ran while one was open for 0% of the time, Pallas kernels for 0%

commit v1 on v0

--- a/solution.py
+++ b/solution.py
@@ -28,7 +28,8 @@
     solution = jnp.zeros_like(base)
     for step in range(blocks):
         residue = (base - lower).astype(jnp.bfloat16)
-        residue_full = lax.all_gather(residue, "col", axis=1, tiled=True)
+        parts = lax.all_gather(residue, "col")
+        residue_full = jnp.concatenate(parts, axis=1)
         pieces = lax.all_to_all(residue_full, "rhs", split_axis=1, concat_axis=0, tiled=True)
         product = jnp.dot(pieces, inverse[0], preferred_element_type=jnp.float32)
         current = lax.psum_scatter(product, "rhs", scatter_dimension=0, tiled=True)

time: 151 us -> 151 us (level)
  no operation moved by 1% of the time
where the time goes in v1:
time: 151 us; the launch traced here: 150 us
  blocking collectives  72.7 us (48%)
  waiting for transfers between devices  43 us (28%)
  matrix products  15.5 us (10%)
  between operations  13.4 us (9%)
  starting transfers between devices  3.3 us (2%)
  local copies, waits for them, and re-layouts  1.76 us (1%)
    reduce_scatter x2, waiting for transfers between devices, body(): current = lax.psum_scatter(product, 'rhs', scatter_dimension=0, tiled=True)  39.2 us
    all_to_all x2, blocking collectives, body(): lax.all_to_all(residue_full, 'rhs', split_axis=1, concat_axis=0, tiled=True)  26.1 us
    psum x1, blocking collectives, body(): shared = lax.psum(coef, ('row', 'col')).astype(jnp.bfloat16)  22.3 us
    psum x1, blocking collectives, body(): old_sum = lax.psum(partial_value, 'col').astype(jnp.bfloat16)  12.7 us
    dot_general x2, matrix products, body(): product = jnp.dot(pieces, inverse[0], preferred_element_type=jnp.float32)  11.6 us
    all_gather x2, blocking collectives, body(): parts = lax.all_gather(residue, 'col')  11.6 us
    all_to_all x1, waiting for transfers between devices, body(): lax.all_to_all(old_sum, 'row', split_axis=0, concat_axis=0, tiled=True)  3.71 us
    all_to_all x1, starting transfers between devices, body(): lax.all_to_all(old_sum, 'row', split_axis=0, concat_axis=0, tiled=True)  3.22 us
  transfers between devices with their start and end apart: 3, of which 3 were waited for; matrix products, arithmetic and copies ran while one was open for 0% of the time, Pallas kernels for 0%

profile of v1, /device:TPU:0, one launch (start us, length us, event | category | flops | bytes accessed | tf_op | source)
XLA Modules:
  0.0 150.4 jit_solution(9258570014789062642)
XLA Ops:
  6.5 0.0 copy-start
  6.5 0.8 copy.7
  7.4 0.1 compare_convert_fusion
  7.4 0.2 copy-done
  7.6 1.2 fusion.9
  8.8 12.7 %psum.14 = bf16[2,16,64]{2,1,0:T(8,128)(2,1)S(1)} all-reduce(f32[2,16,64]{2,1,0:T(8,128)S(1)} %fusion.9), channel_id=1, replica_groups=mesh['row'=2,'col'=4,'rhs'=4] {'col'}, use_global_device_ids=true, to_apply=%region_0.1 | all-reduce | flops 2048 | bytes 12288 | tf_op jit(solution)/shard_map/psum | solution.py:21
  21.5 0.7 reshape.32
  22.2 3.2 %all-to-all-start = ((bf16[2,2,512]{2,1,0:T(2,128)(2,1)}), bf16[2,2,512]{2,1,0:T(2,128)(2,1)S(1)}, u32[]{:S(2)}, u32[]{:S(2)}) async-start(bf16[2,2,512]{2,1,0:T(2,128)(2,1)} %reshape.32), calls=%async_computation | async-start | bytes 8192 | tf_op jit(solution)/shard_map/all_to_all | solution.py:22
  25.4 0.0 reduce-scatter.3.cloned.1.call-start
  25.5 3.7 %all-to-all-done = bf16[2,2,512]{2,1,0:T(2,128)(2,1)S(1)} async-done(((bf16[2,2,512]{2,1,0:T(2,128)(2,1)}), bf16[2,2,512]{2,1,0:T(2,128)(2,1)S(1)}, u32[]{:S(2)}, u32[]{:S(2)}) %all-to-all-start) | async-done | bytes 4128 | tf_op jit(solution)/shard_map/all_to_all | solution.py:22
  29.2 0.1 reshape.33
  29.3 1.4 fusion.26
  30.7 5.8 %all-gather = bf16[64,2048]{1,0:T(8,128)(2,1)S(1)} all-gather(bf16[16,2048]{1,0:T(8,128)(2,1)S(1)} %get-tuple-element.7), channel_id=2, replica_groups=mesh['row'=2,'col'=4,'rhs'=4] {'col'}, dimensions={0}, use_global_device_ids=true | all-gather | bytes 327680 | tf_op jit(solution)/shard_map/all_gather | solution.py:31
  36.5 14.0 %all_to_all.37 = bf16[16,4,2048]{2,0,1:T(8,128)(2,1)S(1)} all-to-all(bf16[16,4,2048]{2,0,1:T(8,128)(2,1)S(1)} %bitcast.60), channel_id=1, replica_groups=mesh['row'=2,'col'=4,'rhs'=4] {'rhs'}, dimensions={1} | all-to-all | bytes 524288 | tf_op jit(solution)/shard_map/all_to_all | solution.py:33
  50.5 0.0 copy-start.1
  50.5 5.8 %fusion.2 = f32[64,2048]{1,0:T(8,128)} fusion(bf16[64,2048]{1,0:T(8,128)(2,1)S(1)} %bitcast.58, bf16[1,2048,2048]{2,1,0:T(8,128)(2,1)} %param.8), kind=kOutput, calls=%fused_computation.2 | convolution fusion | flops 536870912 | bytes 9175040 | tf_op jit(solution)/shard_map/dot_general | solution.py:34
  56.3 0.0 reduce-scatter.3.cloned.1.call-update
  56.3 0.0 reduce-scatter.5.cloned.1.call-start
  56.4 19.2 %reduce-scatter.3.cloned.1.call-done = f32[16,2048]{1,0:T(8,128)} async-done(((f32[64,2048]{1,0:T(8,128)}), f32[16,2048]{1,0:T(8,128)}) %reduce-scatter.3.cloned.1.call-update) | async-done | bytes 131088 | tf_op jit(solution)/shard_map/reduce_scatter | solution.py:35
  75.6 1.2 fusion.8
  76.8 22.3 %psum.15 = bf16[2,16,64]{2,1,0:T(8,128)(2,1)S(1)} all-reduce(f32[2,16,64]{2,1,0:T(8,128)S(1)} %fusion.8), channel_id=1, replica_groups=mesh['row'=2,'col'=4,'rhs'=4] {'row','col'}, use_global_device_ids=true, to_apply=%region_2.3 | all-reduce | flops 2048 | bytes 12288 | tf_op jit(solution)/shard_map/psum | solution.py:46
  99.1 0.0 copy-done.1
  99.1 0.2 fusion.6
  99.3 5.8 %all-gather.1 = bf16[64,2048]{1,0:T(8,128)(2,1)S(1)} all-gather(bf16[16,2048]{1,0:T(8,128)(2,1)S(1)} %fusion.6), channel_id=3, replica_groups=mesh['row'=2,'col'=4,'rhs'=4] {'col'}, dimensions={0}, use_global_device_ids=true | all-gather | bytes 327680 | tf_op jit(solution)/shard_map/all_gather | solution.py:31
  105.1 12.0 %all_to_all.38 = bf16[16,4,2048]{2,0,1:T(8,128)(2,1)S(1)} all-to-all(bf16[16,4,2048]{2,0,1:T(8,128)(2,1)S(1)} %bitcast.61), channel_id=1, replica_groups=mesh['row'=2,'col'=4,'rhs'=4] {'rhs'}, dimensions={1} | all-to-all | bytes 524288 | tf_op jit(solution)/shard_map/all_to_all | solution.py:33
  117.1 0.0 copy-start.2
  117.1 5.8 %fusion = f32[64,2048]{1,0:T(8,128)} fusion(bf16[64,2048]{1,0:T(8,128)(2,1)S(1)} %bitcast.59, bf16[1,2048,2048]{2,1,0:T(8,128)(2,1)} %param.8), kind=kOutput, calls=%fused_computation | convolution fusion | flops 536870912 | bytes 9175040 | tf_op jit(solution)/shard_map/dot_general | solution.py:34
  122.9 0.0 reduce-scatter.5.cloned.1.call-update
  122.9 20.0 %reduce-scatter.5.cloned.1.call-done = f32[16,2048]{1,0:T(8,128)} async-done(((f32[64,2048]{1,0:T(8,128)}), f32[16,2048]{1,0:T(8,128)}) %reduce-scatter.5.cloned.1.call-update) | async-done | bytes 131088 | tf_op jit(solution)/shard_map/reduce_scatter | solution.py:35
  142.9 0.0 copy-done.2
  142.9 0.7 select_bitcast_fusion
  (2 shorter events, 0.0 us)
Async XLA Ops:
  6.5 1.1 copy-start
  22.2 7.0 %all-to-all-start = ((bf16[2,2,512]{2,1,0:T(2,128)(2,1)}), bf16[2,2,512]{2,1,0:T(2,128)(2,1)S(1)}, u32[]{:S(2)}, u32[]{:S(2)}) async-start(bf16[2,2,512]{2,1,0:T(2,128)(2,1)} %reshape.32), calls=%async_computation | async-start | bytes 8192 | tf_op jit(solution)/shard_map/all_to_all | solution.py:22
  25.4 50.1 %reduce-scatter.3.cloned.1.call-start = ((), (), s32[]{:S(2)}) async-start(), calls=%async_computation.5 | async-start | bytes 655360 | tf_op jit(solution)/shard_map/reduce_scatter | solution.py:35
  50.5 48.6 %copy-start.1 = (bf16[1,2,64,2048]{3,2,1,0:T(8,128)(2,1)S(1)}, bf16[1,2,64,2048]{3,2,1,0:T(8,128)(2,1)}, u32[]{:S(2)}) copy-start(bf16[1,2,64,2048]{3,2,1,0:T(8,128)(2,1)} %param.9) | copy-start | bytes 1572868
  56.3 86.6 %reduce-scatter.5.cloned.1.call-start = ((), (), s32[]{:S(2)}) async-start(), calls=%async_computation.6 | async-start | bytes 655360 | tf_op jit(solution)/shard_map/reduce_scatter | solution.py:35
  117.1 25.8 %copy-start.2 = (f32[16,2048]{1,0:T(8,128)S(1)}, f32[16,2048]{1,0:T(8,128)}, u32[]{:S(2)}) copy-start(f32[16,2048]{1,0:T(8,128)} %reduce-scatter.3.cloned.1.call-done) | copy-start | bytes 393220
Sparse Core Ops, SparseCore 0:
  56.4 19.0 reduce-scatter.2
  123.0 19.8 reduce-scatter.4
